TPU v7x, 32 devices: a whole 2x2x4 slice. The times are simulated.
32 devices in a mesh: dp: 4 (over y, x), ctx: 8 (over z, core).
Axes of the slice: x: 2, y: 2, z: 4, core: 2. Of those that a mesh axis runs over, the one named last changes fastest.
Arguments:
- inputs: float32 [4, 1024, 1088], P('dp', 'ctx'), may hold values from -6 to 6
- out_grad: float32 [4, 1024, 1088], P('dp', 'ctx'), may hold values from -6 to 6
- pair_blocks: int32 [8, 2], replicated, may hold values from 0 to 15, as said below
- triple_weight: float32 [1088, 3264], P('ctx', 'dp')
- merge_weight: float32 [1088, 1088], P('ctx', 'dp'), may hold values from -0.75 to 0.75
- expand_weight: float32 [1088, 4352], P('ctx', 'dp'), may hold values from -0.1875 to 0.1875
- shrink_weight: float32 [4352, 1088], P('ctx', 'dp'), may hold values from -0.09375 to 0.09375
- vector_params: float32 [1088, 12], P('ctx', 'dp')
- triple_moment: float32 [1088, 3264], P('ctx', 'dp'), may hold values from -24 to 24
- merge_moment: float32 [1088, 1088], P('ctx', 'dp'), may hold values from -6 to 6
- expand_moment: float32 [1088, 4352], P('ctx', 'dp'), may hold values from -6 to 6
- shrink_moment: float32 [4352, 1088], P('ctx', 'dp'), may hold values from -6 to 6
- vector_moment: float32 [1088, 12], P('ctx', 'dp'), may hold values from -112 to 112
- triple_square: float32 [1088, 3264], P('ctx', 'dp'), may hold values from 24.576 to 245.76
- merge_square: float32 [1088, 1088], P('ctx', 'dp'), may hold values from 8.192 to 81.92
- expand_square: float32 [1088, 4352], P('ctx', 'dp'), may hold values from 8.192 to 81.92
- shrink_square: float32 [4352, 1088], P('ctx', 'dp'), may hold values from 8.192 to 81.92
- vector_square: float32 [1088, 12], P('ctx', 'dp'), may hold values from 204.8 to 2048
Outputs:
- block_output: float32 [4, 1024, 1088], P('dp', 'ctx')
- input_grad: float32 [4, 1024, 1088], P('dp', 'ctx')
- triple_grad: float32 [1088, 3264], P('ctx', 'dp')
- merge_grad: float32 [1088, 1088], P('ctx', 'dp')
- expand_grad: float32 [1088, 4352], P('ctx', 'dp')
- shrink_grad: float32 [4352, 1088], P('ctx', 'dp')
- vector_grad: float32 [1088, 12], P('ctx', 'dp')
- triple_new: float32 [1088, 3264], P('ctx', 'dp')
- merge_new: float32 [1088, 1088], P('ctx', 'dp')
- expand_new: float32 [1088, 4352], P('ctx', 'dp')
- shrink_new: float32 [4352, 1088], P('ctx', 'dp')
- vector_new: float32 [1088, 12], P('ctx', 'dp')
- triple_moment_new: float32 [1088, 3264], P('ctx', 'dp')
- merge_moment_new: float32 [1088, 1088], P('ctx', 'dp')
- expand_moment_new: float32 [1088, 4352], P('ctx', 'dp')
- shrink_moment_new: float32 [4352, 1088], P('ctx', 'dp')
- vector_moment_new: float32 [1088, 12], P('ctx', 'dp')
- triple_square_new: float32 [1088, 3264], P('ctx', 'dp')
- merge_square_new: float32 [1088, 1088], P('ctx', 'dp')
- expand_square_new: float32 [1088, 4352], P('ctx', 'dp')
- shrink_square_new: float32 [4352, 1088], P('ctx', 'dp')
- vector_square_new: float32 [1088, 12], P('ctx', 'dp')
Inputs may be any that keep to these rules, and one draw needn't show every extreme that they name: `pair_blocks`: row c names the two blocks of 64 positions that stand in stored rows c * 2 * 64 onward: first a block p, then 2 * 8 - 1 - p; each of the 16 blocks is named once.
All inputs are finite; a program needn't handle non-finite values.
Results may differ from a plain program's by a relative error of at most 0.011.
Values may be sent and summed in bfloat16 or wider, within the bound.
A program may use at most 256 MiB of HBM per device.

v0:
```python
import jax
import jax.numpy as jnp
from jax import lax
from jax.sharding import PartitionSpec as P

D = 1088
H = 17
HD = 64
BLK = 64
norm_eps = 1e-05
beta_first = 0.9
beta_second = 0.95
learn_rate = 0.01
decay_rate = 0.1
adam_eps = 1e-08
adam_steps = 4
gelu_coef = 0.7978845608028654
masked_score = -1e30


def layer_norm(values):
    center = jnp.mean(values, axis=-1, keepdims=True)
    shifted = values - center
    inverse = lax.rsqrt(jnp.mean(shifted * shifted, axis=-1, keepdims=True) + norm_eps)
    return (shifted * inverse, inverse)


def norm_back(incoming, normed, inverse, gain_vec):
    scaled = incoming * gain_vec
    return inverse * (
        scaled
        - jnp.mean(scaled, axis=-1, keepdims=True)
        - normed * jnp.mean(scaled * normed, axis=-1, keepdims=True)
    )


def gelu_value(values):
    inside = gelu_coef * (values + 0.044715 * values * values * values)
    return 0.5 * values * (1.0 + jnp.tanh(inside))


def gelu_slope(values):
    inside = gelu_coef * (values + 0.044715 * values * values * values)
    tangent = jnp.tanh(inside)
    return 0.5 * (1.0 + tangent) + 0.5 * values * (1.0 - tangent * tangent) * gelu_coef * (
        1.0 + 3.0 * 0.044715 * values * values
    )


def adam_update(weight, gradient, moment, square, decayed):
    moment_new = beta_first * moment + (1.0 - beta_first) * gradient
    square_new = beta_second * square + (1.0 - beta_second) * gradient * gradient
    first_fix = 1.0 - beta_first**adam_steps
    second_fix = 1.0 - beta_second**adam_steps
    direction = moment_new / first_fix / (jnp.sqrt(square_new / second_fix) + adam_eps)
    if decayed:
        direction = direction + decay_rate * weight
    return (weight - learn_rate * direction, moment_new, square_new)


def split_heads(values):
    return values.reshape(values.shape[0], H, HD).transpose(1, 0, 2)


def join_heads(values):
    return values.transpose(1, 0, 2).reshape(values.shape[1], H * HD)


def gather_params(first_part, second_part, third_part, fourth_part, fifth_part):
    piece_one, piece_two, piece_three, piece_four, piece_five = (
        lax.all_gather(first_part, "ctx", axis=0, tiled=True),
        lax.all_gather(second_part, "ctx", axis=0, tiled=True),
        lax.all_gather(third_part, "ctx", axis=0, tiled=True),
        lax.all_gather(fourth_part, "ctx", axis=0, tiled=True),
        lax.all_gather(fifth_part, "ctx", axis=0, tiled=True),
    )
    return (
        lax.all_gather(piece_one, "dp", axis=1, tiled=True),
        lax.all_gather(piece_two, "dp", axis=1, tiled=True),
        lax.all_gather(piece_three, "dp", axis=1, tiled=True),
        lax.all_gather(piece_four, "dp", axis=1, tiled=True),
        lax.all_gather(piece_five, "dp", axis=1, tiled=True),
    )


def reduce_grads(first_part, second_part, third_part, fourth_part, fifth_part):
    piece_one, piece_two, piece_three, piece_four, piece_five = (
        lax.psum_scatter(first_part, "ctx", scatter_dimension=0, tiled=True),
        lax.psum_scatter(second_part, "ctx", scatter_dimension=0, tiled=True),
        lax.psum_scatter(third_part, "ctx", scatter_dimension=0, tiled=True),
        lax.psum_scatter(fourth_part, "ctx", scatter_dimension=0, tiled=True),
        lax.psum_scatter(fifth_part, "ctx", scatter_dimension=0, tiled=True),
    )
    return (
        lax.psum_scatter(piece_one, "dp", scatter_dimension=1, tiled=True),
        lax.psum_scatter(piece_two, "dp", scatter_dimension=1, tiled=True),
        lax.psum_scatter(piece_three, "dp", scatter_dimension=1, tiled=True),
        lax.psum_scatter(piece_four, "dp", scatter_dimension=1, tiled=True),
        lax.psum_scatter(piece_five, "dp", scatter_dimension=1, tiled=True),
    )


def gather_keys(key_rows, value_rows):
    return (
        lax.all_gather(key_rows, "ctx", axis=0, tiled=True),
        lax.all_gather(value_rows, "ctx", axis=0, tiled=True),
    )


def local(
    inputs,
    out_grad,
    pair_blocks,
    triple_weight,
    merge_weight,
    expand_weight,
    shrink_weight,
    vector_params,
    triple_moment,
    merge_moment,
    expand_moment,
    shrink_moment,
    vector_moment,
    triple_square,
    merge_square,
    expand_square,
    shrink_square,
    vector_square,
):
    rows_here = inputs.shape[1]
    stream = inputs[0]
    cotangent = out_grad[0]
    offsets = jnp.arange(BLK, dtype=jnp.int32)
    all_positions = (pair_blocks.reshape(-1)[:, None] * BLK + offsets[None, :]).reshape(-1)
    query_positions = lax.dynamic_slice_in_dim(
        all_positions, lax.axis_index("ctx") * rows_here, rows_here
    )
    allowed = query_positions[:, None] >= all_positions[None, :]
    score_scale = HD ** (-0.5)
    copy_triple = triple_weight.astype(jnp.bfloat16)
    copy_merge = merge_weight.astype(jnp.bfloat16)
    copy_expand = expand_weight.astype(jnp.bfloat16)
    copy_shrink = shrink_weight.astype(jnp.bfloat16)
    copy_vector = vector_params.astype(jnp.bfloat16)
    w_triple, w_merge, w_expand, w_shrink, w_vector = gather_params(
        copy_triple, copy_merge, copy_expand, copy_shrink, copy_vector
    )
    vectors = w_vector.astype(jnp.float32)
    gain_one = vectors[:, 0]
    shift_one = vectors[:, 1]
    query_bias = vectors[:, 2]
    value_bias = vectors[:, 3]
    merge_bias = vectors[:, 4]
    gain_two = vectors[:, 5]
    shift_two = vectors[:, 6]
    shrink_bias = vectors[:, 7]
    expand_bias = vectors[:, 8:12].T.reshape(-1)
    normed_one, inverse_one = layer_norm(stream)
    act_one = (normed_one * gain_one + shift_one).astype(jnp.bfloat16)
    triple = jnp.dot(act_one, w_triple, preferred_element_type=jnp.float32)
    query_b = (triple[:, :D] + query_bias).astype(jnp.bfloat16)
    key_b = triple[:, D : 2 * D].astype(jnp.bfloat16)
    value_b = (triple[:, 2 * D :] + value_bias).astype(jnp.bfloat16)
    keys_all, values_all = gather_keys(key_b, value_b)

    def head_scores(query_h, key_h):
        scores = (
            lax.dot_general(
                query_h, key_h, (((1,), (1,)), ((), ())), preferred_element_type=jnp.float32
            )
            * score_scale
        )
        return jnp.where(allowed, scores, masked_score)

    def head_forward(operands):
        query_h, key_h, value_h = operands
        scores = head_scores(query_h, key_h)
        row_max = jnp.max(scores, axis=1, keepdims=True)
        log_total = row_max + jnp.log(jnp.sum(jnp.exp(scores - row_max), axis=1, keepdims=True))
        probs_b = jnp.exp(scores - log_total).astype(jnp.bfloat16)
        attended = jnp.dot(probs_b, value_h, preferred_element_type=jnp.float32)
        return (attended.astype(jnp.bfloat16), log_total[:, 0])

    heads_query = split_heads(query_b)
    heads_key = split_heads(keys_all)
    heads_value = split_heads(values_all)
    heads_out, heads_total = lax.map(head_forward, (heads_query, heads_key, heads_value))
    attended_b = join_heads(heads_out)
    middle = stream + jnp.dot(attended_b, w_merge, preferred_element_type=jnp.float32) + merge_bias
    normed_two, inverse_two = layer_norm(middle)
    act_two = (normed_two * gain_two + shift_two).astype(jnp.bfloat16)
    pre_act = jnp.dot(act_two, w_expand, preferred_element_type=jnp.float32) + expand_bias
    hidden_b = gelu_value(pre_act).astype(jnp.bfloat16)
    block_out = (
        middle + jnp.dot(hidden_b, w_shrink, preferred_element_type=jnp.float32) + shrink_bias
    )
    back_triple, back_merge, back_expand, back_shrink, unused_vector = gather_params(
        copy_triple, copy_merge, copy_expand, copy_shrink, copy_vector
    )
    keys_again, values_again = gather_keys(key_b, value_b)
    back_key = split_heads(keys_again)
    back_value = split_heads(values_again)
    cotangent_b = cotangent.astype(jnp.bfloat16)
    shrink_local = jnp.dot(hidden_b.T, cotangent_b, preferred_element_type=jnp.float32)
    shrink_bias_grad = jnp.sum(cotangent, axis=0)
    dpre = jnp.dot(cotangent_b, back_shrink.T, preferred_element_type=jnp.float32) * gelu_slope(
        pre_act
    )
    dpre_b = dpre.astype(jnp.bfloat16)
    expand_local = jnp.dot(act_two.T, dpre_b, preferred_element_type=jnp.float32)
    expand_bias_grad = jnp.sum(dpre, axis=0)
    dact_two = jnp.dot(dpre_b, back_expand.T, preferred_element_type=jnp.float32)
    gain_two_grad = jnp.sum(dact_two * normed_two, axis=0)
    shift_two_grad = jnp.sum(dact_two, axis=0)
    dmiddle = cotangent + norm_back(dact_two, normed_two, inverse_two, gain_two)
    dmiddle_b = dmiddle.astype(jnp.bfloat16)
    merge_local = jnp.dot(attended_b.T, dmiddle_b, preferred_element_type=jnp.float32)
    merge_bias_grad = jnp.sum(dmiddle, axis=0)
    dattended_b = jnp.dot(dmiddle_b, back_merge.T, preferred_element_type=jnp.float32).astype(
        jnp.bfloat16
    )

    def head_backward(operands):
        query_h, key_h, value_h, out_h, dout_h, log_total = operands
        scores = head_scores(query_h, key_h)
        probs = jnp.exp(scores - log_total[:, None])
        probs_b = probs.astype(jnp.bfloat16)
        delta = jnp.sum(
            dout_h.astype(jnp.float32) * out_h.astype(jnp.float32), axis=1, keepdims=True
        )
        dprobs = lax.dot_general(
            dout_h, value_h, (((1,), (1,)), ((), ())), preferred_element_type=jnp.float32
        )
        dscores_b = (probs * (dprobs - delta) * score_scale).astype(jnp.bfloat16)
        dquery_h = jnp.dot(dscores_b, key_h, preferred_element_type=jnp.float32)
        dkey_h = lax.dot_general(
            dscores_b, query_h, (((0,), (0,)), ((), ())), preferred_element_type=jnp.float32
        )
        dvalue_h = lax.dot_general(
            probs_b, dout_h, (((0,), (0,)), ((), ())), preferred_element_type=jnp.float32
        )
        return (dquery_h, dkey_h, dvalue_h)

    dquery_heads, dkey_heads, dvalue_heads = lax.map(
        head_backward,
        (heads_query, back_key, back_value, heads_out, split_heads(dattended_b), heads_total),
    )
    dquery = join_heads(dquery_heads)
    dkey_rows, dvalue_rows = (
        lax.psum_scatter(join_heads(dkey_heads), "ctx", scatter_dimension=0, tiled=True),
        lax.psum_scatter(join_heads(dvalue_heads), "ctx", scatter_dimension=0, tiled=True),
    )
    dtriple_b = jnp.concatenate([dquery, dkey_rows, dvalue_rows], axis=1).astype(jnp.bfloat16)
    triple_local = jnp.dot(act_one.T, dtriple_b, preferred_element_type=jnp.float32)
    query_bias_grad = jnp.sum(dquery, axis=0)
    value_bias_grad = jnp.sum(dvalue_rows, axis=0)
    dact_one = jnp.dot(dtriple_b, back_triple.T, preferred_element_type=jnp.float32)
    gain_one_grad = jnp.sum(dact_one * normed_one, axis=0)
    shift_one_grad = jnp.sum(dact_one, axis=0)
    input_rows = dmiddle + norm_back(dact_one, normed_one, inverse_one, gain_one)
    vector_local = jnp.concatenate(
        [
            jnp.stack(
                [
                    gain_one_grad,
                    shift_one_grad,
                    query_bias_grad,
                    value_bias_grad,
                    merge_bias_grad,
                    gain_two_grad,
                    shift_two_grad,
                    shrink_bias_grad,
                ],
                axis=1,
            ),
            expand_bias_grad.reshape(4, D).T,
        ],
        axis=1,
    )
    triple_grad, merge_grad, expand_grad, shrink_grad, vector_grad = reduce_grads(
        triple_local, merge_local, expand_local, shrink_local, vector_local
    )
    triple_new, triple_moment_new, triple_square_new = adam_update(
        triple_weight, triple_grad, triple_moment, triple_square, True
    )
    merge_new, merge_moment_new, merge_square_new = adam_update(
        merge_weight, merge_grad, merge_moment, merge_square, True
    )
    expand_new, expand_moment_new, expand_square_new = adam_update(
        expand_weight, expand_grad, expand_moment, expand_square, True
    )
    shrink_new, shrink_moment_new, shrink_square_new = adam_update(
        shrink_weight, shrink_grad, shrink_moment, shrink_square, True
    )
    vector_new, vector_moment_new, vector_square_new = adam_update(
        vector_params, vector_grad, vector_moment, vector_square, False
    )
    return (
        block_out[None],
        input_rows[None],
        triple_grad,
        merge_grad,
        expand_grad,
        shrink_grad,
        vector_grad,
        triple_new,
        merge_new,
        expand_new,
        shrink_new,
        vector_new,
        triple_moment_new,
        merge_moment_new,
        expand_moment_new,
        shrink_moment_new,
        vector_moment_new,
        triple_square_new,
        merge_square_new,
        expand_square_new,
        shrink_square_new,
        vector_square_new,
    )


def solution(mesh):
    in_specs = (
        P("dp", "ctx", None),
        P("dp", "ctx", None),
        P(),
        P("ctx", "dp"),
        P("ctx", "dp"),
        P("ctx", "dp"),
        P("ctx", "dp"),
        P("ctx", "dp"),
        P("ctx", "dp"),
        P("ctx", "dp"),
        P("ctx", "dp"),
        P("ctx", "dp"),
        P("ctx", "dp"),
        P("ctx", "dp"),
        P("ctx", "dp"),
        P("ctx", "dp"),
        P("ctx", "dp"),
        P("ctx", "dp"),
    )
    out_specs = (
        P("dp", "ctx", None),
        P("dp", "ctx", None),
        P("ctx", "dp"),
        P("ctx", "dp"),
        P("ctx", "dp"),
        P("ctx", "dp"),
        P("ctx", "dp"),
        P("ctx", "dp"),
        P("ctx", "dp"),
        P("ctx", "dp"),
        P("ctx", "dp"),
        P("ctx", "dp"),
        P("ctx", "dp"),
        P("ctx", "dp"),
        P("ctx", "dp"),
        P("ctx", "dp"),
        P("ctx", "dp"),
        P("ctx", "dp"),
        P("ctx", "dp"),
        P("ctx", "dp"),
        P("ctx", "dp"),
        P("ctx", "dp"),
    )
    return jax.shard_map(local, mesh=mesh, in_specs=in_specs, out_specs=out_specs, check_vma=False)
```

profile of v0, /device:TPU:0, one launch (start us, length us, event | category | flops | bytes accessed | tf_op | source)
XLA Modules:
  0.0 1586.2 jit_solution(11072138455714467575)
XLA Ops:
  9.1 31.8 %all-gather.13.cloned.1.call-done = bf16[1088,816]{1,0:T(8,128)(2,1)} async-done(((bf16[136,816]{1,0:T(8,128)(2,1)}), bf16[1088,816]{1,0:T(8,128)(2,1)}) %all-gather.13.cloned.1.call-update) | async-done | bytes 1775632 | tf_op jit(solution)/shard_map/all_gather | solution.py:71
  40.9 4.0 copy.90
  46.9 12.8 all-gather
  59.8 8.8 all-gather.1
  69.6 55.4 %all-gather.15.cloned.1.call-done = bf16[1088,3264]{0,1:T(8,128)(2,1)} async-done(((bf16[1088,816]{0,1:T(8,128)(2,1)}), bf16[1088,3264]{0,1:T(8,128)(2,1)}) %all-gather.15.cloned.1.call-update) | async-done | bytes 7102480 | tf_op jit(solution)/shard_map/all_gather | solution.py:78
  125.0 5.4 fusion.75
  132.6 21.3 %all_gather.52 = bf16[1088,272]{1,0:T(8,128)(2,1)S(1)} all-gather(bf16[136,272]{1,0:T(8,128)(2,1)S(1)} %convert_element_type.74), channel_id=1, replica_groups=mesh['dp'=4,'ctx'=8] {'ctx'}, dimensions={0}, use_global_device_ids=true | all-gather | bytes 665856 | tf_op jit(solution)/shard_map/all_gather | solution.py:72
  155.0 11.0 all-gather.23.cloned.1.call-done
  166.0 5.1 copy.96
  173.4 28.5 %all-gather.29.cloned.1.call-done = bf16[8,544,272]{1,2,0:T(8,128)(2,1)} async-done(((bf16[1,544,272]{1,2,0:T(8,128)(2,1)}), bf16[8,544,272]{1,2,0:T(8,128)(2,1)}) %all-gather.29.cloned.1.call-update) | async-done | bytes 2367504 | tf_op jit(solution)/shard_map/all_gather | solution.py:74
  204.3 3.1 reshape.198
  208.6 26.0 %all-gather.17.cloned.1.call-done = bf16[1024,1088]{0,1:T(8,128)(2,1)} async-done(((bf16[128,1088]{0,1:T(8,128)(2,1)}), bf16[1024,1088]{0,1:T(8,128)(2,1)}) %all-gather.17.cloned.1.call-update) | async-done | bytes 2228240 | tf_op jit(solution)/shard_map/all_gather | solution.py:105
  234.7 5.2 copy.92
  239.9 27.4 %all-gather.19.cloned.1.call-done = bf16[1024,1088]{0,1:T(8,128)(2,1)} async-done(((bf16[128,1088]{0,1:T(8,128)(2,1)}), bf16[1024,1088]{0,1:T(8,128)(2,1)}) %all-gather.19.cloned.1.call-update) | async-done | bytes 2228240 | tf_op jit(solution)/shard_map/all_gather | solution.py:106
  267.3 5.3 copy.93
  272.6 69.9 %while.28 = (s32[]{:T(128)}, bf16[17,128,64]{1,2,0:T(8,128)(2,1)S(1)}, f32[17,128]{1,0:T(8,128)}, bf16[17,128,64]{2,1,0:T(8,128)(2,1)S(1)}, bf16[17,1024,64]{2,1...) while((s32[]{:T(128)}, ...), condition=%wide.region_5.6_spmd.clone, body=%wide.region_2.5_spmd.clone.sunk | while | flops 34611072 | bytes 2157681 | solution.py:187
  343.3 2.5 fusion.86
  346.6 63.8 %all-gather.25.cloned.1.call-done = bf16[1088,4352]{0,1:T(8,128)(2,1)} async-done(((bf16[1088,1088]{0,1:T(8,128)(2,1)}), bf16[1088,4352]{0,1:T(8,128)(2,1)}) %all-gather.25.cloned.1.call-update) | async-done | bytes 9469968 | tf_op jit(solution)/shard_map/all_gather | solution.py:80
  410.4 7.3 convolution_add_fusion
  417.6 91.1 %all-gather.27.cloned.1.call-done = bf16[4352,1088]{0,1:T(8,128)(2,1)} async-done(((bf16[4352,272]{0,1:T(8,128)(2,1)}), bf16[4352,1088]{0,1:T(8,128)(2,1)}) %all-gather.27.cloned.1.call-update) | async-done | bytes 9469968 | tf_op jit(solution)/shard_map/all_gather | solution.py:81
  508.8 7.5 fusion.87
  516.3 4.9 multiply_reduce_fusion
  523.8 133.4 %while.29 = (s32[]{:T(128)}, f32[17,128,64]{1,2,0:T(8,128)}, f32[17,1024,64]{1,2,0:T(8,128)}, f32[17,1024,64]{1,2,0:T(8,128)}, bf16[17,128,64]{2,1,0:T(8,128)(2,...) while((s32[]{:T(128)}, f32[17,128,64]{1,2,0:T(8,128)}, ...), condition=%wide.region_12.13_spmd.clone, body=%wide.region_10.12_spmd.clone.sunk | while | flops 85098368 | bytes 3944593 | solution.py:244
  658.1 3.0 fusion.69
  662.7 9.6 fusion.68
  674.2 35.6 %reduce-scatter.20.cloned.1.call-done = f32[128,1088]{0,1:T(8,128)} async-done(((f32[1024,1088]{0,1:T(8,128)}), f32[128,1088]{0,1:T(8,128)}) %reduce-scatter.20.cloned.1.call-update) | async-done | bytes 557072 | tf_op jit(solution)/shard_map/reduce_scatter | solution.py:250
  711.6 51.4 %reduce-scatter.22.cloned.1.call-done = f32[128,1088]{0,1:T(8,128)} async-done(((f32[1024,1088]{0,1:T(8,128)}), f32[128,1088]{0,1:T(8,128)}) %reduce-scatter.22.cloned.1.call-update) | async-done | bytes 557072 | tf_op jit(solution)/shard_map/reduce_scatter | solution.py:251
  765.8 8.5 fusion.65
  774.9 9.5 fusion.59
  784.5 37.1 %reduce-scatter.36.cloned.1.call-done = f32[136,1088]{1,0:T(8,128)} async-done(((f32[1088,1088]{1,0:T(8,128)}), f32[136,1088]{1,0:T(8,128)}) %reduce-scatter.36.cloned.1.call-update) | async-done | bytes 591888
  821.6 2.4 copy.110
  824.1 197.3 %reduce-scatter.28.cloned.1.call-done = f32[544,1088]{1,0:T(8,128)} async-done(((f32[4352,1088]{1,0:T(8,128)}), f32[544,1088]{1,0:T(8,128)}) %reduce-scatter.28.cloned.1.call-update) | async-done | bytes 2367504 | tf_op jit(solution)/shard_map/reduce_scatter | solution.py:91
  1021.5 147.7 %reduce-scatter.24.cloned.1.call-done = f32[136,3264]{1,0:T(8,128)} async-done(((f32[1088,3264]{1,0:T(8,128)}), f32[136,3264]{1,0:T(8,128)}) %reduce-scatter.24.cloned.1.call-update) | async-done | bytes 1775632 | tf_op jit(solution)/shard_map/reduce_scatter | solution.py:88
  1169.2 3.4 copy.108
  1172.7 186.2 %reduce-scatter.26.cloned.1.call-done = f32[136,4352]{1,0:T(8,128)} async-done(((f32[1088,4352]{1,0:T(8,128)}), f32[136,4352]{1,0:T(8,128)}) %reduce-scatter.26.cloned.1.call-update) | async-done | bytes 2367504 | tf_op jit(solution)/shard_map/reduce_scatter | solution.py:90
  1358.9 5.0 copy.112
  1370.5 2.4 copy.101
  1386.5 7.3 fusion.49
  1394.0 7.2 multiply_reduce_fusion.1
  1402.6 28.0 %all-reduce.2 = f32[1088,12]{0,1:T(8,128)} all-reduce(f32[1088,12]{0,1:T(8,128)} %concatenate.8), channel_id=12, replica_groups=mesh['dp'=4,'ctx'=8] {'ctx'}, use_global_device_ids=true, to_apply=%region_34.35.clone | all-reduce | flops 13056 | bytes 104448
  1432.0 17.5 %all-reduce.3 = f32[136,12]{0,1:T(8,128)} all-reduce(f32[136,12]{0,1:T(8,128)} %constant_dynamic-slice_fusion.2), channel_id=13, replica_groups=mesh['dp'=4,'ctx'=8] {'dp'}, use_global_device_ids=true, to_apply=%region_35.36.clone | all-reduce | flops 1632 | bytes 13056
  1457.1 11.4 all-reduce.6.cloned.1.call-done
  1468.5 3.9 multiply_subtract_fusion
  1472.4 2.4 copy.104
  1479.5 37.7 %reduce-scatter.30.cloned.1.call-done = f32[816,136]{1,0:T(8,128)} async-done(((f32[3264,136]{1,0:T(8,128)}), f32[816,136]{1,0:T(8,128)}) %reduce-scatter.30.cloned.1.call-update) | async-done | bytes 443920
  1518.6 2.7 multiply_subtract_fusion.2
  1521.3 53.7 %reduce-scatter.34.cloned.1.call-done = f32[1088,136]{1,0:T(8,128)} async-done(((f32[4352,136]{1,0:T(8,128)}), f32[1088,136]{1,0:T(8,128)}) %reduce-scatter.34.cloned.1.call-update) | async-done | bytes 591888
  1576.6 2.9 multiply_subtract_fusion.1
  (461 shorter events, 266.3 us)
Async XLA Ops:
  7.2 33.7 %all-gather.13.cloned.1.call-start = ((), (), s32[]{:S(2)}) async-start(), calls=%async_computation.9 | async-start | bytes 2193408 | tf_op jit(solution)/shard_map/all_gather | solution.py:71
  9.0 35.9 %copy-start.14 = (f32[136,1088]{1,0:T(8,128)S(1)}, f32[136,1088]{1,0:T(8,128)}, u32[]{:S(2)}) copy-start(f32[136,1088]{1,0:T(8,128)} %param.27) | copy-start | bytes 1775620
  9.0 116.0 %all-gather.15.cloned.1.call-start = ((), (), s32[]{:S(2)}) async-start(), calls=%async_computation.10 | async-start | bytes 9400320 | tf_op jit(solution)/shard_map/all_gather | solution.py:78
  44.9 23.7 %copy-start.1 = (f32[1,128,1088]{1,2,0:T(8,128)S(1)}, f32[1,128,1088]{1,2,0:T(8,128)}, u32[]{:S(2)}) copy-start(f32[1,128,1088]{1,2,0:T(8,128)} %param.22) | copy-start | bytes 1671172
  44.9 121.1 %all-gather.23.cloned.1.call-start = ((), (), s32[]{:S(2)}) async-start(), calls=%async_computation.14 | async-start | bytes 2820096 | tf_op jit(solution)/shard_map/all_gather | solution.py:73
  45.7 156.2 %all-gather.29.cloned.1.call-start = ((), (), s32[]{:S(2)}) async-start(), calls=%async_computation.22 | async-start | bytes 3133440 | tf_op jit(solution)/shard_map/all_gather | solution.py:74
  46.9 187.8 %all-gather.17.cloned.1.call-start = ((), (), s32[]{:S(2)}) async-start(), calls=%async_computation.11 | async-start | bytes 2506752 | tf_op jit(solution)/shard_map/all_gather | solution.py:105
  69.4 61.0 %copy-start.32 = (f32[1088]{0:T(1024)}, f32[1088]{0:T(1024)S(1)}, u32[]{:S(2)}) copy-start(f32[1088]{0:T(1024)S(1)} %get-tuple-element.323) | copy-start | bytes 13060
  69.4 61.0 %copy-start.34 = (f32[1088]{0:T(1024)}, f32[1088]{0:T(1024)S(1)}, u32[]{:S(2)}) copy-start(f32[1088]{0:T(1024)S(1)} %get-tuple-element.322) | copy-start | bytes 13060
  69.5 61.0 %copy-start.47 = (f32[128]{0:T(128)}, f32[128]{0:T(128)S(1)}, u32[]{:S(2)}) copy-start(f32[128]{0:T(128)S(1)} %broadcast_multiply_fusion.6) | copy-start | bytes 1540
  69.6 60.8 %copy-start.51 = (f32[128]{0:T(128)}, f32[128]{0:T(128)S(1)}, u32[]{:S(2)}) copy-start(f32[128]{0:T(128)S(1)} %add_rsqrt_fusion.1) | copy-start | bytes 1540
  131.2 136.1 %all-gather.19.cloned.1.call-start = ((), (), s32[]{:S(2)}) async-start(), calls=%async_computation.12 | async-start | bytes 2506752 | tf_op jit(solution)/shard_map/all_gather | solution.py:106
  132.5 210.1 %all-gather.21.cloned.1.call-start = ((), (), s32[]{:S(2)}) async-start(), calls=%async_computation.13 | async-start | bytes 3133440 | tf_op jit(solution)/shard_map/all_gather | solution.py:79
  155.0 255.4 %all-gather.25.cloned.1.call-start = ((), (), s32[]{:S(2)}) async-start(), calls=%async_computation.15 | async-start | bytes 12533760 | tf_op jit(solution)/shard_map/all_gather | solution.py:80
  171.2 337.6 %all-gather.27.cloned.1.call-start = ((), (), s32[]{:S(2)}) async-start(), calls=%async_computation.16 | async-start | bytes 11837440 | tf_op jit(solution)/shard_map/all_gather | solution.py:81
  207.4 502.4 %reduce-scatter.20.cloned.1.call-start = ((), (), s32[]{:S(2)}) async-start(), calls=%async_computation.17 | async-start | bytes 5013504 | tf_op jit(solution)/shard_map/reduce_scatter | solution.py:250
  272.6 70.7 %copy-start.37 = (f32[1088]{0:T(1024)S(1)}, f32[1088]{0:T(1024)}, u32[]{:S(2)}) copy-start(f32[1088]{0:T(1024)} %get-tuple-element.319) | copy-start | bytes 13060
  345.9 64.5 %copy-start.38 = (f32[128]{0:T(128)}, f32[128]{0:T(128)S(1)}, u32[]{:S(2)}) copy-start(f32[128]{0:T(128)S(1)} %broadcast_multiply_fusion.5) | copy-start | bytes 1540
  417.6 98.6 %copy-start.3 = (f32[128,4352]{1,0:T(8,128)}, f32[128,4352]{1,0:T(8,128)S(1)}, u32[]{:S(2)}) copy-start(f32[128,4352]{1,0:T(8,128)S(1)} %convolution_add_fusion) | copy-start | bytes 6684676
  508.7 7.5 copy-start
  508.7 7.5 copy-start.31
  508.7 7.5 copy-start.39
  508.7 7.5 copy-start.41
  522.2 135.8 %copy-start.5 = (f32[128,1088]{0,1:T(8,128)}, f32[128,1088]{0,1:T(8,128)S(1)}, u32[]{:S(2)}) copy-start(f32[128,1088]{0,1:T(8,128)S(1)} %get-tuple-element.382) | copy-start | bytes 1671172
  657.3 105.8 %reduce-scatter.22.cloned.1.call-start = ((), (), s32[]{:S(2)}) async-start(), calls=%async_computation.18 | async-start | bytes 5013504 | tf_op jit(solution)/shard_map/reduce_scatter | solution.py:251
  658.0 163.6 %reduce-scatter.36.cloned.1.call-start = ((), (), s32[]{:S(2)}) async-start(), calls=%async_computation.27 | async-start | bytes 5640192
  661.1 360.4 %reduce-scatter.28.cloned.1.call-start = ((), (), s32[]{:S(2)}) async-start(), calls=%async_computation.21 | async-start | bytes 22560768 | tf_op jit(solution)/shard_map/reduce_scatter | solution.py:91
  672.3 93.5 %copy-start.48 = (f32[128]{0:T(128)S(1)}, f32[128]{0:T(128)}, u32[]{:S(2)}) copy-start(f32[128]{0:T(128)} %copy-done.47) | copy-start | bytes 1540
  672.3 496.9 %reduce-scatter.24.cloned.1.call-start = ((), (), s32[]{:S(2)}) async-start(), calls=%async_computation.19 | async-start | bytes 16293888 | tf_op jit(solution)/shard_map/reduce_scatter | solution.py:88
  774.3 584.6 %reduce-scatter.26.cloned.1.call-start = ((), (), s32[]{:S(2)}) async-start(), calls=%async_computation.20 | async-start | bytes 21307392 | tf_op jit(solution)/shard_map/reduce_scatter | solution.py:90
  784.5 669.4 %reduce-scatter.32.cloned.1.call-start = ((), (), s32[]{:S(2)}) async-start(), calls=%async_computation.24 | async-start | bytes 1392640
  824.1 644.4 %all-reduce.6.cloned.1.call-start = ((), (), s32[]{:S(2)}) async-start(), calls=%async_computation.26 | async-start | bytes 5013504
  1021.5 495.7 %reduce-scatter.30.cloned.1.call-start = ((), (), s32[]{:S(2)}) async-start(), calls=%async_computation.23 | async-start | bytes 4177920
  1172.7 402.3 %reduce-scatter.34.cloned.1.call-start = ((), (), s32[]{:S(2)}) async-start(), calls=%async_computation.25 | async-start | bytes 5570560
  1363.9 11.5 copy-start.56
  1386.5 7.4 copy-start.25
  1386.5 7.4 copy-start.27
  1386.5 7.4 copy-start.33
  1386.5 7.4 copy-start.49
  1386.5 7.4 copy-start.52
  1394.0 58.2 %copy-start.6 = (f32[128,1088]{0,1:T(8,128)S(1)}, f32[128,1088]{0,1:T(8,128)}, u32[]{:S(2)}) copy-start(f32[128,1088]{0,1:T(8,128)} %copy-done.5) | copy-start | bytes 1671172
  1402.6 66.0 %copy-start.9 = (f32[544,272]{1,0:T(8,128)S(1)}, f32[544,272]{1,0:T(8,128)}, u32[]{:S(2)}) copy-start(f32[544,272]{1,0:T(8,128)} %copy.103) | copy-start | bytes 1775620
  1402.6 66.0 %copy-start.10 = (f32[544,272]{1,0:T(8,128)S(1)}, f32[544,272]{1,0:T(8,128)}, u32[]{:S(2)}) copy-start(f32[544,272]{1,0:T(8,128)} %copy.100) | copy-start | bytes 1775620
  1455.0 17.4 %copy-start.29 = (f32[136,272]{1,0:T(8,128)}, f32[136,272]{1,0:T(8,128)S(1)}, u32[]{:S(2)}) copy-start(f32[136,272]{1,0:T(8,128)S(1)} %copy.111) | copy-start | bytes 443908
  1477.1 41.4 %copy-start.18 = (f32[136,816]{1,0:T(8,128)S(1)}, f32[136,816]{1,0:T(8,128)}, u32[]{:S(2)}) copy-start(f32[136,816]{1,0:T(8,128)} %param.25) | copy-start | bytes 1331716
  1518.6 58.0 %copy-start.17 = (f32[136,816]{1,0:T(8,128)}, f32[136,816]{1,0:T(8,128)S(1)}, u32[]{:S(2)}) copy-start(f32[136,816]{1,0:T(8,128)S(1)} %copy.109) | copy-start | bytes 1331716
  1518.6 58.0 %copy-start.15 = (f32[136,1088]{1,0:T(8,128)S(1)}, f32[136,1088]{1,0:T(8,128)}, u32[]{:S(2)}) copy-start(f32[136,1088]{1,0:T(8,128)} %param.27) | copy-start | bytes 1775620
  1518.6 58.0 %copy-start.30 = (f32[136,1088]{1,0:T(8,128)S(1)}, f32[136,1088]{1,0:T(8,128)}, u32[]{:S(2)}) copy-start(f32[136,1088]{1,0:T(8,128)} %param.32) | copy-start | bytes 1775620
  (28 other events, 115.5 us)
Sparse Core Ops, SparseCore 0:
  10.2 30.6 all-gather.12
  45.0 79.9 all-gather.14
  127.2 38.7 all-gather.22
  168.1 33.8 all-gather.28
  203.9 30.6 all-gather.16
  236.7 30.5 all-gather.18
  269.7 37.5 all-gather.20
  309.2 101.1 all-gather.24
  412.2 96.4 all-gather.26
  657.4 52.3 reduce-scatter.19
  712.1 50.8 reduce-scatter.21
  765.2 56.3 reduce-scatter.35
  824.0 197.4 reduce-scatter.27
  1023.6 145.5 reduce-scatter.23
  1171.4 187.4 reduce-scatter.25
  1361.7 26.8 reduce-scatter.31
  1391.6 76.8 all-reduce.5
  1471.4 45.6 reduce-scatter.29
  1520.2 54.7 reduce-scatter.33
where the time goes:
time: 1600 us; the launch traced here: 1590 us
  waiting for transfers between devices  1090 us (68%)
  matrix products  234 us (15%)
  local copies, waits for them, and re-layouts  113 us (7%)
  blocking collectives  88.3 us (6%)
  other arithmetic  38.1 us (2%)
  between operations  16.8 us (1%)
    reduce_scatter x1, waiting for transfers between devices, reduce_grads(): lax.psum_scatter(fourth_part, 'ctx', scatter_dimension=0, tiled=True)  197 us
    reduce_scatter x1, waiting for transfers between devices, reduce_grads(): lax.psum_scatter(third_part, 'ctx', scatter_dimension=0, tiled=True)  186 us
    reduce_scatter x1, waiting for transfers between devices, reduce_grads(): lax.psum_scatter(first_part, 'ctx', scatter_dimension=0, tiled=True)  148 us
    unnamed x24, waiting for transfers between devices  141 us
    all_gather x1, waiting for transfers between devices, gather_params(): lax.all_gather(piece_four, 'dp', axis=1, tiled=True)  91.1 us
    all_gather x1, waiting for transfers between devices, gather_params(): lax.all_gather(piece_three, 'dp', axis=1, tiled=True)  63.8 us
    all_gather x1, waiting for transfers between devices, gather_params(): lax.all_gather(piece_one, 'dp', axis=1, tiled=True)  55.4 us
    reduce_scatter x1, waiting for transfers between devices, local(): lax.psum_scatter(join_heads(dvalue_heads), 'ctx', scatter_dimension=0, ti...  51.4 us
  transfers between devices with their start and end apart: 19, of which 17 were waited for; matrix products, arithmetic and copies ran while one was open for 14% of the time, Pallas kernels for 0%

commit v1 on v0

--- a/solution.py
+++ b/solution.py
@@ -18,6 +18,11 @@
 masked_score = -1e30
 
 
+def gather_over(x, axis, along):
+    sent = jnp.stack([x] * lax.axis_size(axis))
+    return jnp.concatenate(lax.all_to_all(sent, axis, 0, 0), axis=along)
+
+
 def layer_norm(values):
     center = jnp.mean(values, axis=-1, keepdims=True)
     shifted = values - center
@@ -78,7 +83,7 @@
         lax.all_gather(piece_one, "dp", axis=1, tiled=True),
         lax.all_gather(piece_two, "dp", axis=1, tiled=True),
         lax.all_gather(piece_three, "dp", axis=1, tiled=True),
-        lax.all_gather(piece_four, "dp", axis=1, tiled=True),
+        gather_over(piece_four, "dp", 1),
         lax.all_gather(piece_five, "dp", axis=1, tiled=True),
     )
 

time: 1600 us -> 1520 us (0.950)
  waiting for transfers between devices: 1090 us -> 1000 us
    all_gather x1 -> x0, waiting for transfers between devices: 91.1 us -> none  [gather_params(): lax.all_gather(piece_four, 'dp', axis=1, tiled=True)]
    all_gather x1, waiting for transfers between devices: 28.5 us -> 11.6 us  [gather_params(): lax.all_gather(fourth_part, 'ctx', axis=0, tiled=True)]
    unnamed x24 -> x23, waiting for transfers between devices: 141 us -> 141 us
  transfers between devices with their start and end apart: 19 -> 19, of which waited for: 17 -> 16; matrix products, arithmetic and copies ran while one was open for 14% -> 15% of each run, Pallas kernels for 0% -> 0%
where the time goes in v1:
time: 1520 us; the launch traced here: 1510 us
  waiting for transfers between devices  1000 us (66%)
  matrix products  235 us (15%)
  local copies, waits for them, and re-layouts  118 us (8%)
  blocking collectives  88.3 us (6%)
  other arithmetic  38.1 us (3%)
  between operations  17.2 us (1%)
    reduce_scatter x1, waiting for transfers between devices, reduce_grads(): lax.psum_scatter(fourth_part, 'ctx', scatter_dimension=0, tiled=True)  197 us
    reduce_scatter x1, waiting for transfers between devices, reduce_grads(): lax.psum_scatter(third_part, 'ctx', scatter_dimension=0, tiled=True)  186 us
    reduce_scatter x1, waiting for transfers between devices, reduce_grads(): lax.psum_scatter(first_part, 'ctx', scatter_dimension=0, tiled=True)  148 us
    unnamed x23, waiting for transfers between devices  141 us
    all_gather x1, waiting for transfers between devices, gather_params(): lax.all_gather(piece_three, 'dp', axis=1, tiled=True)  73.3 us
    all_gather x1, waiting for transfers between devices, gather_params(): lax.all_gather(piece_one, 'dp', axis=1, tiled=True)  55.4 us
    reduce_scatter x1, waiting for transfers between devices, local(): lax.psum_scatter(join_heads(dvalue_heads), 'ctx', scatter_dimension=0, ti...  51.3 us
    unnamed x2, blocking collectives  45.5 us
  transfers between devices with their start and end apart: 19, of which 16 were waited for; matrix products, arithmetic and copies ran while one was open for 15% of the time, Pallas kernels for 0%

profile of v1, /device:TPU:0, one launch (start us, length us, event | category | flops | bytes accessed | tf_op | source)
XLA Modules:
  0.0 1505.2 jit_solution(719009018444153431)
XLA Ops:
  9.1 31.8 %all-gather.12.cloned.1.call-done = bf16[1088,816]{1,0:T(8,128)(2,1)} async-done(((bf16[136,816]{1,0:T(8,128)(2,1)}), bf16[1088,816]{1,0:T(8,128)(2,1)}) %all-gather.12.cloned.1.call-update) | async-done | bytes 1775632 | tf_op jit(solution)/shard_map/all_gather | solution.py:76
  40.9 3.9 copy.90
  46.9 12.8 all-gather
  59.7 8.8 all-gather.1
  69.6 55.4 %all-gather.14.cloned.1.call-done = bf16[1088,3264]{0,1:T(8,128)(2,1)} async-done(((bf16[1088,816]{0,1:T(8,128)(2,1)}), bf16[1088,3264]{0,1:T(8,128)(2,1)}) %all-gather.14.cloned.1.call-update) | async-done | bytes 7102480 | tf_op jit(solution)/shard_map/all_gather | solution.py:83
  125.0 5.4 fusion.77
  132.5 21.2 %all_gather.48 = bf16[1088,272]{1,0:T(8,128)(2,1)S(1)} all-gather(bf16[136,272]{1,0:T(8,128)(2,1)S(1)} %convert_element_type.79), channel_id=1, replica_groups=mesh['dp'=4,'ctx'=8] {'ctx'}, dimensions={0}, use_global_device_ids=true | all-gather | bytes 665856 | tf_op jit(solution)/shard_map/all_gather | solution.py:77
  156.6 11.6 all-gather.26.cloned.1.call-done
  170.6 3.0 reshape.211
  173.6 5.9 stack.36
  179.6 5.8 all-to-all-start
  185.4 16.3 %all-gather.22.cloned.1.call-done = bf16[1088,1088]{1,0:T(8,128)(2,1)} async-done(((bf16[136,1088]{1,0:T(8,128)(2,1)}), bf16[1088,1088]{1,0:T(8,128)(2,1)}) %all-gather.22.cloned.1.call-update) | async-done | bytes 2367504 | tf_op jit(solution)/shard_map/all_gather | solution.py:78
  201.7 5.1 copy.96
  208.2 26.4 %all-gather.16.cloned.1.call-done = bf16[1024,1088]{0,1:T(8,128)(2,1)} async-done(((bf16[128,1088]{0,1:T(8,128)(2,1)}), bf16[1024,1088]{0,1:T(8,128)(2,1)}) %all-gather.16.cloned.1.call-update) | async-done | bytes 2228240 | tf_op jit(solution)/shard_map/all_gather | solution.py:110
  234.6 5.2 copy.92
  239.8 27.1 %all-gather.18.cloned.1.call-done = bf16[1024,1088]{0,1:T(8,128)(2,1)} async-done(((bf16[128,1088]{0,1:T(8,128)(2,1)}), bf16[1024,1088]{0,1:T(8,128)(2,1)}) %all-gather.18.cloned.1.call-update) | async-done | bytes 2228240 | tf_op jit(solution)/shard_map/all_gather | solution.py:111
  267.0 5.3 copy.93
  272.2 69.9 %while.28 = (s32[]{:T(128)}, bf16[17,128,64]{1,2,0:T(8,128)(2,1)S(1)}, f32[17,128]{1,0:T(8,128)}, bf16[17,128,64]{2,1,0:T(8,128)(2,1)S(1)}, bf16[17,1024,64]{2,1...) while((s32[]{:T(128)}, ...), condition=%wide.region_5.6_spmd.clone, body=%wide.region_2.5_spmd.clone.sunk | while | flops 34611072 | bytes 2157681 | solution.py:192
  343.0 2.5 fusion.87
  346.2 73.3 %all-gather.24.cloned.1.call-done = bf16[1088,4352]{0,1:T(8,128)(2,1)} async-done(((bf16[1088,1088]{0,1:T(8,128)(2,1)}), bf16[1088,4352]{0,1:T(8,128)(2,1)}) %all-gather.24.cloned.1.call-update) | async-done | bytes 9469968 | tf_op jit(solution)/shard_map/all_gather | solution.py:85
  419.6 7.3 convolution_add_fusion
  426.9 8.2 fusion.88
  435.1 4.9 multiply_reduce_fusion
  442.6 133.4 %while.29 = (s32[]{:T(128)}, f32[17,128,64]{1,2,0:T(8,128)}, f32[17,1024,64]{1,2,0:T(8,128)}, f32[17,1024,64]{1,2,0:T(8,128)}, bf16[17,128,64]{2,1,0:T(8,128)(2,...) while((s32[]{:T(128)}, f32[17,128,64]{1,2,0:T(8,128)}, ...), condition=%wide.region_12.13_spmd.clone, body=%wide.region_10.12_spmd.clone.sunk | while | flops 85098368 | bytes 3944593 | solution.py:249
  576.7 3.0 fusion.71
  581.4 9.7 fusion.67
  593.0 35.7 %reduce-scatter.20.cloned.1.call-done = f32[128,1088]{0,1:T(8,128)} async-done(((f32[1024,1088]{0,1:T(8,128)}), f32[128,1088]{0,1:T(8,128)}) %reduce-scatter.20.cloned.1.call-update) | async-done | bytes 557072 | tf_op jit(solution)/shard_map/reduce_scatter | solution.py:255
  630.4 51.3 %reduce-scatter.22.cloned.1.call-done = f32[128,1088]{0,1:T(8,128)} async-done(((f32[1024,1088]{0,1:T(8,128)}), f32[128,1088]{0,1:T(8,128)}) %reduce-scatter.22.cloned.1.call-update) | async-done | bytes 557072 | tf_op jit(solution)/shard_map/reduce_scatter | solution.py:256
  684.5 8.5 fusion.65
  693.6 9.5 fusion.59
  703.2 37.2 %reduce-scatter.36.cloned.1.call-done = f32[136,1088]{1,0:T(8,128)} async-done(((f32[1088,1088]{1,0:T(8,128)}), f32[136,1088]{1,0:T(8,128)}) %reduce-scatter.36.cloned.1.call-update) | async-done | bytes 591888
  740.4 2.4 copy.110
  743.0 197.2 %reduce-scatter.28.cloned.1.call-done = f32[544,1088]{1,0:T(8,128)} async-done(((f32[4352,1088]{1,0:T(8,128)}), f32[544,1088]{1,0:T(8,128)}) %reduce-scatter.28.cloned.1.call-update) | async-done | bytes 2367504 | tf_op jit(solution)/shard_map/reduce_scatter | solution.py:96
  940.2 147.8 %reduce-scatter.24.cloned.1.call-done = f32[136,3264]{1,0:T(8,128)} async-done(((f32[1088,3264]{1,0:T(8,128)}), f32[136,3264]{1,0:T(8,128)}) %reduce-scatter.24.cloned.1.call-update) | async-done | bytes 1775632 | tf_op jit(solution)/shard_map/reduce_scatter | solution.py:93
  1088.0 3.4 copy.108
  1091.5 186.3 %reduce-scatter.26.cloned.1.call-done = f32[136,4352]{1,0:T(8,128)} async-done(((f32[1088,4352]{1,0:T(8,128)}), f32[136,4352]{1,0:T(8,128)}) %reduce-scatter.26.cloned.1.call-update) | async-done | bytes 2367504 | tf_op jit(solution)/shard_map/reduce_scatter | solution.py:95
  1277.8 5.0 copy.112
  1305.4 7.3 fusion.49
  1312.9 7.2 multiply_reduce_fusion.1
  1321.5 28.0 %all-reduce.2 = f32[1088,12]{0,1:T(8,128)} all-reduce(f32[1088,12]{0,1:T(8,128)} %concatenate.8), channel_id=12, replica_groups=mesh['dp'=4,'ctx'=8] {'ctx'}, use_global_device_ids=true, to_apply=%region_34.35.clone | all-reduce | flops 13056 | bytes 104448
  1350.9 17.5 %all-reduce.3 = f32[136,12]{0,1:T(8,128)} all-reduce(f32[136,12]{0,1:T(8,128)} %constant_dynamic-slice_fusion.2), channel_id=13, replica_groups=mesh['dp'=4,'ctx'=8] {'dp'}, use_global_device_ids=true, to_apply=%region_35.36.clone | all-reduce | flops 1632 | bytes 13056
  1376.0 11.3 all-reduce.6.cloned.1.call-done
  1387.3 3.9 multiply_subtract_fusion
  1391.2 2.4 copy.104
  1398.3 37.7 %reduce-scatter.30.cloned.1.call-done = f32[816,136]{1,0:T(8,128)} async-done(((f32[3264,136]{1,0:T(8,128)}), f32[816,136]{1,0:T(8,128)}) %reduce-scatter.30.cloned.1.call-update) | async-done | bytes 443920
  1437.4 2.7 multiply_subtract_fusion.2
  1440.1 53.6 %reduce-scatter.34.cloned.1.call-done = f32[1088,136]{1,0:T(8,128)} async-done(((f32[4352,136]{1,0:T(8,128)}), f32[1088,136]{1,0:T(8,128)}) %reduce-scatter.34.cloned.1.call-update) | async-done | bytes 591888
  1495.3 2.9 multiply_subtract_fusion.1
  (461 shorter events, 267.9 us)
Async XLA Ops:
  7.2 33.7 %all-gather.12.cloned.1.call-start = ((), (), s32[]{:S(2)}) async-start(), calls=%async_computation.10 | async-start | bytes 2193408 | tf_op jit(solution)/shard_map/all_gather | solution.py:76
  9.0 35.9 %copy-start.13 = (f32[544,272]{0,1:T(8,128)S(1)}, f32[544,272]{0,1:T(8,128)}, u32[]{:S(2)}) copy-start(f32[544,272]{0,1:T(8,128)} %param.28) | copy-start | bytes 1775620
  9.0 115.9 %all-gather.14.cloned.1.call-start = ((), (), s32[]{:S(2)}) async-start(), calls=%async_computation.11 | async-start | bytes 9400320 | tf_op jit(solution)/shard_map/all_gather | solution.py:83
  44.8 23.7 %copy-start.1 = (f32[1,128,1088]{1,2,0:T(8,128)S(1)}, f32[1,128,1088]{1,2,0:T(8,128)}, u32[]{:S(2)}) copy-start(f32[1,128,1088]{1,2,0:T(8,128)} %param.22) | copy-start | bytes 1671172
  44.9 123.4 %all-gather.26.cloned.1.call-start = ((), (), s32[]{:S(2)}) async-start(), calls=%async_computation.22 | async-start | bytes 3133440 | tf_op jit(solution)/shard_map/all_gather | solution.py:79
  45.7 156.0 %all-gather.22.cloned.1.call-start = ((), (), s32[]{:S(2)}) async-start(), calls=%async_computation.15 | async-start | bytes 2820096 | tf_op jit(solution)/shard_map/all_gather | solution.py:78
  46.8 187.8 %all-gather.16.cloned.1.call-start = ((), (), s32[]{:S(2)}) async-start(), calls=%async_computation.12 | async-start | bytes 2506752 | tf_op jit(solution)/shard_map/all_gather | solution.py:110
  69.4 61.0 %copy-start.32 = (f32[1088]{0:T(1024)}, f32[1088]{0:T(1024)S(1)}, u32[]{:S(2)}) copy-start(f32[1088]{0:T(1024)S(1)} %get-tuple-element.323) | copy-start | bytes 13060
  69.4 61.0 %copy-start.34 = (f32[1088]{0:T(1024)}, f32[1088]{0:T(1024)S(1)}, u32[]{:S(2)}) copy-start(f32[1088]{0:T(1024)S(1)} %get-tuple-element.322) | copy-start | bytes 13060
  69.4 61.1 %copy-start.47 = (f32[128]{0:T(128)}, f32[128]{0:T(128)S(1)}, u32[]{:S(2)}) copy-start(f32[128]{0:T(128)S(1)} %broadcast_multiply_fusion.6) | copy-start | bytes 1540
  69.5 60.9 %copy-start.51 = (f32[128]{0:T(128)}, f32[128]{0:T(128)S(1)}, u32[]{:S(2)}) copy-start(f32[128]{0:T(128)S(1)} %add_rsqrt_fusion.1) | copy-start | bytes 1540
  131.2 135.7 %all-gather.18.cloned.1.call-start = ((), (), s32[]{:S(2)}) async-start(), calls=%async_computation.13 | async-start | bytes 2506752 | tf_op jit(solution)/shard_map/all_gather | solution.py:111
  132.4 22.6 %copy-start.55 = (s32[8,2]{0,1:T(2,128)S(1)}, s32[8,2]{0,1:T(2,128)}, u32[]{:S(2)}) copy-start(s32[8,2]{0,1:T(2,128)} %param.24) | copy-start | bytes 196
  132.4 209.7 %all-gather.20.cloned.1.call-start = ((), (), s32[]{:S(2)}) async-start(), calls=%async_computation.14 | async-start | bytes 3133440 | tf_op jit(solution)/shard_map/all_gather | solution.py:84
  179.6 247.3 %all-to-all-start = ((bf16[4,4352,272]{1,2,0:T(8,128)(2,1)}), bf16[4,4352,272]{1,2,0:T(8,128)(2,1)}, u32[]{:S(2)}, u32[]{:S(2)}) async-start(bf16[4,4352,272]{1,2,0:T(8,128)(2,1)} %stack.36), calls=%async_computation | async-start | bytes 18939904 | tf_op jit(solution)/shard_map/all_to_all | solution.py:23
  185.4 234.2 %all-gather.24.cloned.1.call-start = ((), (), s32[]{:S(2)}) async-start(), calls=%async_computation.16 | async-start | bytes 12533760 | tf_op jit(solution)/shard_map/all_gather | solution.py:85
  206.9 421.7 %reduce-scatter.20.cloned.1.call-start = ((), (), s32[]{:S(2)}) async-start(), calls=%async_computation.17 | async-start | bytes 5013504 | tf_op jit(solution)/shard_map/reduce_scatter | solution.py:255
  272.2 70.7 %copy-start.37 = (f32[1088]{0:T(1024)S(1)}, f32[1088]{0:T(1024)}, u32[]{:S(2)}) copy-start(f32[1088]{0:T(1024)} %get-tuple-element.319) | copy-start | bytes 13060
  345.5 74.0 %copy-start.38 = (f32[128]{0:T(128)}, f32[128]{0:T(128)S(1)}, u32[]{:S(2)}) copy-start(f32[128]{0:T(128)S(1)} %broadcast_multiply_fusion.5) | copy-start | bytes 1540
  426.8 8.2 copy-start.3
  426.8 8.2 copy-start
  426.8 8.2 copy-start.31
  426.9 8.2 copy-start.39
  426.9 8.2 copy-start.41
  441.0 135.7 %copy-start.5 = (f32[128,1088]{0,1:T(8,128)}, f32[128,1088]{0,1:T(8,128)S(1)}, u32[]{:S(2)}) copy-start(f32[128,1088]{0,1:T(8,128)S(1)} %get-tuple-element.382) | copy-start | bytes 1671172
  576.1 105.6 %reduce-scatter.22.cloned.1.call-start = ((), (), s32[]{:S(2)}) async-start(), calls=%async_computation.18 | async-start | bytes 5013504 | tf_op jit(solution)/shard_map/reduce_scatter | solution.py:256
  576.7 163.8 %reduce-scatter.36.cloned.1.call-start = ((), (), s32[]{:S(2)}) async-start(), calls=%async_computation.27 | async-start | bytes 5640192
  579.8 360.4 %reduce-scatter.28.cloned.1.call-start = ((), (), s32[]{:S(2)}) async-start(), calls=%async_computation.21 | async-start | bytes 22560768 | tf_op jit(solution)/shard_map/reduce_scatter | solution.py:96
  591.1 93.4 %copy-start.48 = (f32[128]{0:T(128)S(1)}, f32[128]{0:T(128)}, u32[]{:S(2)}) copy-start(f32[128]{0:T(128)} %copy-done.47) | copy-start | bytes 1540
  591.1 496.9 %reduce-scatter.24.cloned.1.call-start = ((), (), s32[]{:S(2)}) async-start(), calls=%async_computation.19 | async-start | bytes 16293888 | tf_op jit(solution)/shard_map/reduce_scatter | solution.py:93
  693.0 584.8 %reduce-scatter.26.cloned.1.call-start = ((), (), s32[]{:S(2)}) async-start(), calls=%async_computation.20 | async-start | bytes 21307392 | tf_op jit(solution)/shard_map/reduce_scatter | solution.py:95
  703.2 669.6 %reduce-scatter.32.cloned.1.call-start = ((), (), s32[]{:S(2)}) async-start(), calls=%async_computation.24 | async-start | bytes 1392640
  742.9 644.4 %all-reduce.6.cloned.1.call-start = ((), (), s32[]{:S(2)}) async-start(), calls=%async_computation.26 | async-start | bytes 5013504
  940.2 495.8 %reduce-scatter.30.cloned.1.call-start = ((), (), s32[]{:S(2)}) async-start(), calls=%async_computation.23 | async-start | bytes 4177920
  1091.5 402.2 %reduce-scatter.34.cloned.1.call-start = ((), (), s32[]{:S(2)}) async-start(), calls=%async_computation.25 | async-start | bytes 5570560
  1282.8 11.5 copy-start.56
  1305.4 7.4 copy-start.27
  1305.4 7.4 copy-start.33
  1305.4 7.4 copy-start.49
  1305.4 7.4 copy-start.52
  1312.8 58.2 %copy-start.6 = (f32[128,1088]{0,1:T(8,128)S(1)}, f32[128,1088]{0,1:T(8,128)}, u32[]{:S(2)}) copy-start(f32[128,1088]{0,1:T(8,128)} %copy-done.5) | copy-start | bytes 1671172
  1321.5 65.9 %copy-start.9 = (f32[544,272]{1,0:T(8,128)S(1)}, f32[544,272]{1,0:T(8,128)}, u32[]{:S(2)}) copy-start(f32[544,272]{1,0:T(8,128)} %copy.103) | copy-start | bytes 1775620
  1321.5 65.9 %copy-start.10 = (f32[544,272]{1,0:T(8,128)S(1)}, f32[544,272]{1,0:T(8,128)}, u32[]{:S(2)}) copy-start(f32[544,272]{1,0:T(8,128)} %copy.100) | copy-start | bytes 1775620
  1373.9 17.3 %copy-start.29 = (f32[136,272]{1,0:T(8,128)}, f32[136,272]{1,0:T(8,128)S(1)}, u32[]{:S(2)}) copy-start(f32[136,272]{1,0:T(8,128)S(1)} %copy.111) | copy-start | bytes 443908
  1396.0 41.4 %copy-start.18 = (f32[136,816]{1,0:T(8,128)S(1)}, f32[136,816]{1,0:T(8,128)}, u32[]{:S(2)}) copy-start(f32[136,816]{1,0:T(8,128)} %param.25) | copy-start | bytes 1331716
  1437.4 57.9 %copy-start.17 = (f32[136,816]{1,0:T(8,128)}, f32[136,816]{1,0:T(8,128)S(1)}, u32[]{:S(2)}) copy-start(f32[136,816]{1,0:T(8,128)S(1)} %copy.109) | copy-start | bytes 1331716
  1437.4 57.9 %copy-start.15 = (f32[136,1088]{1,0:T(8,128)S(1)}, f32[136,1088]{1,0:T(8,128)}, u32[]{:S(2)}) copy-start(f32[136,1088]{1,0:T(8,128)} %param.27) | copy-start | bytes 1775620
  1437.4 57.9 %copy-start.30 = (f32[136,1088]{1,0:T(8,128)S(1)}, f32[136,1088]{1,0:T(8,128)}, u32[]{:S(2)}) copy-start(f32[136,1088]{1,0:T(8,128)} %param.32) | copy-start | bytes 1775620
  (28 other events, 122.3 us)
Sparse Core Ops, SparseCore 0:
  10.2 30.6 all-gather.11
  45.0 79.9 all-gather.13
  127.2 40.9 all-gather.25
  170.3 31.4 all-gather.21
  203.8 30.8 all-gather.15
  236.6 30.2 all-gather.17
  269.4 47.0 all-gather.19
  318.3 101.2 all-gather.23
  576.2 52.3 reduce-scatter.19
  630.8 50.8 reduce-scatter.21
  684.0 56.3 reduce-scatter.35
  742.7 197.4 reduce-scatter.27
  942.5 145.5 reduce-scatter.23
  1090.2 187.5 reduce-scatter.25
  1280.6 26.7 reduce-scatter.31
  1310.5 76.8 all-reduce.5
  1390.2 45.6 reduce-scatter.29
  1438.9 54.7 reduce-scatter.33
